TPU v7x, 32 devices: a whole 2x2x4 slice. The times are simulated.
32 devices in a mesh: pipe: 2 (over x), expert: 16 (over z, y, core).
Axes of the slice: x: 2, y: 2, z: 4, core: 2. Of those that a mesh axis runs over, the one named last changes fastest.
Arguments:
- inputs: bfloat16 [1, 512, 5120], P(None, 'expert'), may hold values from -6 to 6
- router: bfloat16 [2, 5120, 2], P('pipe'), may hold values from -0.078125 to 0.078125
- w_up: bfloat16 [2, 3072, 5120], P('pipe', 'expert'), may hold values from -0.078125 to 0.078125
- w_down: bfloat16 [2, 3072, 5120], P('pipe', 'expert'), may hold values from -0.15625 to 0.15625
- picks: int32 [2, 1, 2, 8], P('pipe'), may hold values from 0 to 511, as said below
- probe: bfloat16 [2, 64, 5120], P('pipe'), may hold values from -0.078125 to 0.078125
Outputs:
- student_feats: bfloat16 [2, 1, 512, 64], P('pipe', None, 'expert')
Inputs may be any that keep to these rules, and one draw needn't show every extreme that they name: Each list picks[s, m, e] holds 8 different token positions of the micro-batch. Of the 32 consecutive positions held by one index of expert, at most 1 stand in one list, and in every list some index has exactly 1.
All inputs are finite; a program needn't handle non-finite values.
Results may differ from a plain program's by a relative error of at most 0.0059.
Values may be sent and summed in bfloat16 or wider, within the bound.
A program may use at most 64 MiB of HBM per device.

v0:
```python
import jax
import jax.numpy as jnp
from jax import lax
from jax.sharding import PartitionSpec as P

SLOT = 1


def passed_along(x, axis, by):
    size = lax.axis_size(axis)
    pairs = [(i, i + by) for i in range(size) if 0 <= i + by < size]
    return lax.ppermute(x, axis, pairs)


def from_root(x, axis, root):
    mine = lax.axis_index(axis) == root
    return lax.psum(jnp.where(mine, x, jnp.zeros_like(x)), axis)


def rms_rows(rows_in):
    wide = rows_in.astype(jnp.float32)
    scale = lax.rsqrt(jnp.mean(wide * wide, axis=-1, keepdims=True) + 1e-06)
    return (wide * scale).astype(jnp.bfloat16)


def shards(inputs, router, w_up, w_down, picks, probe):
    sections = lax.axis_size("pipe")
    expert_width = lax.axis_size("expert")
    section_index = lax.axis_index("pipe")
    source = lax.axis_index("expert")
    micro_count, tok_rows, features = inputs.shape
    experts = router.shape[2]
    group_size = expert_width // experts
    tick_count = micro_count + sections - 1
    positions = jnp.arange(tok_rows, dtype=jnp.int32)
    slot_ids = jnp.arange(SLOT, dtype=jnp.int32)

    def expert_rows(received):
        row_shape = received.shape
        flat_rows = received.reshape(-1, row_shape[2])
        pre = lax.dot_general(
            flat_rows, w_up[0], (((1,), (1,)), ((), ())), preferred_element_type=jnp.float32
        )
        hidden = jax.nn.silu(pre).astype(jnp.bfloat16)
        partials = jnp.dot(hidden, w_down[0], preferred_element_type=jnp.float32).astype(
            jnp.bfloat16
        )
        return partials.reshape(row_shape)

    def layer(rows_in, micro_index):
        normed = rms_rows(rows_in)
        gate_values = jax.nn.sigmoid(jnp.dot(normed, router[0], preferred_element_type=jnp.float32))
        chosen = lax.dynamic_index_in_dim(picks[0], micro_index, 0, keepdims=False)
        local_rows = chosen - source * tok_rows
        owned = (local_rows >= 0) & (local_rows < tok_rows)
        owned_count = owned.astype(jnp.int32)
        slot_place = jnp.cumsum(owned_count, axis=1) - owned_count
        slot_hot = ((slot_place[:, :, None] == slot_ids) & owned[:, :, None]).astype(jnp.bfloat16)
        row_hot = (local_rows[:, :, None] == positions).astype(jnp.bfloat16)
        selector = jnp.einsum("ecr,ect->ert", slot_hot, row_hot, preferred_element_type=jnp.float32)
        picked = jnp.einsum(
            "ert,td->erd", selector.astype(jnp.bfloat16), normed, preferred_element_type=jnp.float32
        ).astype(jnp.bfloat16)
        copies = jnp.repeat(picked, group_size, axis=0)
        partials = expert_rows(
            lax.all_to_all(copies, "expert", split_axis=0, concat_axis=0, tiled=True)
        )
        returned = lax.all_to_all(partials, "expert", split_axis=0, concat_axis=0, tiled=True)
        expert_out = jnp.sum(
            returned.astype(jnp.float32).reshape(experts, group_size, SLOT, features), axis=1
        )
        weights = selector * jnp.transpose(gate_values)[:, None, :]
        update = jnp.einsum("ert,erd->td", weights, expert_out, precision=lax.Precision.HIGHEST)
        return (rows_in.astype(jnp.float32) + update).astype(jnp.bfloat16)

    def tick(tick_index, loop_state):
        previous, finals = loop_state
        arrived = passed_along(previous, "pipe", 1)
        micro_index = jnp.clip(tick_index - section_index, 0, micro_count - 1)
        fresh_rows = lax.dynamic_index_in_dim(
            inputs, jnp.clip(tick_index, 0, micro_count - 1), 0, keepdims=False
        )
        rows_in = jnp.where(section_index == 0, fresh_rows, arrived)
        result = layer(rows_in, micro_index)
        finished = (
            (section_index == sections - 1)
            & (tick_index - section_index >= 0)
            & (tick_index - section_index < micro_count)
        )
        stored = lax.dynamic_update_index_in_dim(finals, result, micro_index, 0)
        finals = jnp.where(finished, stored, finals)
        return (result, finals)

    start_rows = jnp.zeros((tok_rows, features), jnp.bfloat16)
    start_finals = jnp.zeros((micro_count, tok_rows, features), jnp.bfloat16)
    previous, finals = lax.fori_loop(0, tick_count, tick, (start_rows, start_finals))
    shared = from_root(finals, "pipe", sections - 1)
    final_normed = rms_rows(shared)
    student_rows = jnp.einsum(
        "mtd,jd->mtj", final_normed, probe[0], preferred_element_type=jnp.float32
    )
    return student_rows.astype(jnp.bfloat16)[None]


def solution(mesh):
    return jax.shard_map(
        shards,
        mesh=mesh,
        in_specs=(
            P(None, "expert", None),
            P("pipe", None, None),
            P("pipe", "expert", None),
            P("pipe", "expert", None),
            P("pipe", None, None, None),
            P("pipe", None, None),
        ),
        out_specs=P("pipe", None, "expert", None),
        check_vma=False,
    )
```

profile of v0, /device:TPU:9, one launch (start us, length us, event | category | flops | bytes accessed | tf_op | source)
XLA Modules:
  0.0 136.9 jit_solution(14568044816781589299)
XLA Ops:
  7.7 93.1 %while.21 = (s32[]{:T(128)}, bf16[32,5120]{1,0:T(8,128)(2,1)}, bf16[1,32,5120]{2,1,0:T(8,128)(2,1)}, pred[]{:T(512)}, bf16[1,32,5120]{2,1,0:T(8,128)(2,1)}, /*in...) while((s32[]{:T(128)}, bf16[32,5120]{1,0:T(8,128)(2,1)}, ...), condition=%wide.region_4.5_spmd.clone, body=%wide.region_1.4_spmd.clone.sunk | while | flops 71040296 | bytes 23656336 | solution.py:96
  7.7 3.3 %collective-permute-start = (bf16[32,5120]{1,0:T(8,128)(2,1)S(1)}, bf16[32,5120]{1,0:T(8,128)(2,1)S(1)}, u32[]{:S(2)}, u32[]{:S(2)}) collective-permute-start(bf16[32,5120]{1,0:T(8,128)(2,1)S(1)} %broadcast_select_fusion.3), channel_id=1, source_target_pairs={{0,16},{1,17},{2,18},{3,19},{4,20},{5,21},{6,22},{7,23},{8,24},{9,... | collective-permute-start | bytes 983048 | tf_op jit(solution)/shard_map/while/body/eval_jaxpr/ppermute | solution.py:12
  11.0 6.4 %collective-permute-done = bf16[32,5120]{1,0:T(8,128)(2,1)S(1)} collective-permute-done((bf16[32,5120]{1,0:T(8,128)(2,1)S(1)}, bf16[32,5120]{1,0:T(8,128)(2,1)S(1)}, u32[]{:S(2)}, u32[]{:S(2)}) %collective-permute-start) | collective-permute-done | bytes 327712 | tf_op jit(solution)/shard_map/while/body/eval_jaxpr/ppermute | solution.py:12
  17.4 1.2 fusion.64
  19.4 0.8 reduce.13
  20.3 13.8 %all_to_all.32 = bf16[16,2,2560]{2,1,0:T(2,128)(2,1)S(1)} all-to-all(bf16[16,2,2560]{2,1,0:T(2,128)(2,1)S(1)} %reshape.138), channel_id=1, replica_groups=mesh['pipe'=2,'expert'=16] {'expert'}, dimensions={0} | all-to-all | bytes 327680 | tf_op jit(solution)/shard_map/while/body/eval_jaxpr/all_to_all | solution.py:66
  34.2 3.0 %fusion.66 = bf16[16,1,5120]{2,0,1:T(8,128)(2,1)S(1)} fusion(bf16[1,192,5120]{2,1,0:T(8,128)(2,1)} %get-tuple-element.587, bf16[1,192,5120]{2,1,0:T(8,128)(2,1)S(1)} %copy-done.1, bf16[16,1,5120]{2,1,0:T(2,128)(2,1)S(1)} %reshape.139), kind=kOutput, calls=%fused_computation.3.clone.1 | convolution fusion | flops 63011840 | bytes 4259840 | tf_op jit(solution)/shard_map/while/body/eval_jaxpr/dot_general | solution.py:45
  38.6 0.8 reshape.140
  39.4 5.3 %all-to-all-start.1 = ((bf16[16,2,2560]{2,1,0:T(2,128)(2,1)}), bf16[16,2,2560]{2,1,0:T(2,128)(2,1)S(1)}, u32[]{:S(2)}, u32[]{:S(2)}) async-start(bf16[16,2,2560]{2,1,0:T(2,128)(2,1)} %reshape.140), calls=%async_computation.1 | async-start | bytes 327680 | tf_op jit(solution)/shard_map/while/body/eval_jaxpr/all_to_all | solution.py:68
  45.0 6.3 %all-to-all-done.1 = bf16[16,2,2560]{2,1,0:T(2,128)(2,1)S(1)} async-done(((bf16[16,2,2560]{2,1,0:T(2,128)(2,1)}), bf16[16,2,2560]{2,1,0:T(2,128)(2,1)S(1)}, u32[]{:S(2)}, u32[]{:S(2)}) %all-to-all-start.1) | async-done | bytes 163872 | tf_op jit(solution)/shard_map/while/body/eval_jaxpr/all_to_all | solution.py:68
  51.9 1.6 %bitcast_select_fusion.4 = (bf16[1,32,5120]{2,1,0:T(8,128)(2,1)S(1)}, bf16[32,5120]{1,0:T(8,128)(2,1)}) fusion(bf16[1,32,5120]{2,1,0:T(8,128)(2,1)S(1)} %copy-done.2, pred[]{:T(512)S(6)} %compare.3, pred[]{:T(512)S(6)} %and.69, f32[2,32]{1,0:T(2,128)S(1)} %fusion.67, f32[2,5120]{1,0:T(2,128)S(1)} %bitcast_reduce_fusion.2, ...), kind=kOutput, calls=%fused_computation.20.clone.1 | convolution fusion | flops 4751360 | bytes 1351938 | tf_op jit(solution)/shard_map/while/body/eval_jaxpr/ert,erd->td/dot_general | solution.py:73
  54.2 1.1 broadcast_select_fusion.3
  55.3 4.1 %collective-permute-start = (bf16[32,5120]{1,0:T(8,128)(2,1)S(1)}, bf16[32,5120]{1,0:T(8,128)(2,1)S(1)}, u32[]{:S(2)}, u32[]{:S(2)}) collective-permute-start(bf16[32,5120]{1,0:T(8,128)(2,1)S(1)} %broadcast_select_fusion.3), channel_id=1, source_target_pairs={{0,16},{1,17},{2,18},{3,19},{4,20},{5,21},{6,22},{7,23},{8,24},{9,... | collective-permute-start | bytes 983048 | tf_op jit(solution)/shard_map/while/body/eval_jaxpr/ppermute | solution.py:12
  59.5 7.4 %collective-permute-done = bf16[32,5120]{1,0:T(8,128)(2,1)S(1)} collective-permute-done((bf16[32,5120]{1,0:T(8,128)(2,1)S(1)}, bf16[32,5120]{1,0:T(8,128)(2,1)S(1)}, u32[]{:S(2)}, u32[]{:S(2)}) %collective-permute-start) | collective-permute-done | bytes 327712 | tf_op jit(solution)/shard_map/while/body/eval_jaxpr/ppermute | solution.py:12
  66.8 1.2 fusion.64
  68.9 0.8 reduce.13
  69.8 10.9 %all_to_all.32 = bf16[16,2,2560]{2,1,0:T(2,128)(2,1)S(1)} all-to-all(bf16[16,2,2560]{2,1,0:T(2,128)(2,1)S(1)} %reshape.138), channel_id=1, replica_groups=mesh['pipe'=2,'expert'=16] {'expert'}, dimensions={0} | all-to-all | bytes 327680 | tf_op jit(solution)/shard_map/while/body/eval_jaxpr/all_to_all | solution.py:66
  80.8 3.0 %fusion.66 = bf16[16,1,5120]{2,0,1:T(8,128)(2,1)S(1)} fusion(bf16[1,192,5120]{2,1,0:T(8,128)(2,1)} %get-tuple-element.587, bf16[1,192,5120]{2,1,0:T(8,128)(2,1)S(1)} %copy-done.1, bf16[16,1,5120]{2,1,0:T(2,128)(2,1)S(1)} %reshape.139), kind=kOutput, calls=%fused_computation.3.clone.1 | convolution fusion | flops 63011840 | bytes 4259840 | tf_op jit(solution)/shard_map/while/body/eval_jaxpr/dot_general | solution.py:45
  86.0 5.3 %all-to-all-start.1 = ((bf16[16,2,2560]{2,1,0:T(2,128)(2,1)}), bf16[16,2,2560]{2,1,0:T(2,128)(2,1)S(1)}, u32[]{:S(2)}, u32[]{:S(2)}) async-start(bf16[16,2,2560]{2,1,0:T(2,128)(2,1)} %reshape.140), calls=%async_computation.1 | async-start | bytes 327680 | tf_op jit(solution)/shard_map/while/body/eval_jaxpr/all_to_all | solution.py:68
  91.6 6.3 %all-to-all-done.1 = bf16[16,2,2560]{2,1,0:T(2,128)(2,1)S(1)} async-done(((bf16[16,2,2560]{2,1,0:T(2,128)(2,1)}), bf16[16,2,2560]{2,1,0:T(2,128)(2,1)S(1)}, u32[]{:S(2)}, u32[]{:S(2)}) %all-to-all-start.1) | async-done | bytes 163872 | tf_op jit(solution)/shard_map/while/body/eval_jaxpr/all_to_all | solution.py:68
  98.5 1.6 %bitcast_select_fusion.4 = (bf16[1,32,5120]{2,1,0:T(8,128)(2,1)S(1)}, bf16[32,5120]{1,0:T(8,128)(2,1)}) fusion(bf16[1,32,5120]{2,1,0:T(8,128)(2,1)S(1)} %copy-done.2, pred[]{:T(512)S(6)} %compare.3, pred[]{:T(512)S(6)} %and.69, f32[2,32]{1,0:T(2,128)S(1)} %fusion.67, f32[2,5120]{1,0:T(2,128)S(1)} %bitcast_reduce_fusion.2, ...), kind=kOutput, calls=%fused_computation.20.clone.1 | convolution fusion | flops 4751360 | bytes 1351938 | tf_op jit(solution)/shard_map/while/body/eval_jaxpr/ert,erd->td/dot_general | solution.py:73
  101.6 25.4 %all-reduce.2.cloned.1.call-done = bf16[1,32,5120]{2,1,0:T(8,128)(2,1)} async-done(((bf16[1,32,5120]{2,1,0:T(8,128)(2,1)}), bf16[1,32,5120]{2,1,0:T(8,128)(2,1)}) %all-reduce.2.cloned.1.call-update) | async-done | bytes 327696 | tf_op jit(solution)/shard_map/psum | solution.py:17
  127.0 1.1 fusion.29
  128.1 1.9 %fusion.28 = bf16[1,1,32,64]{3,2,1,0:T(8,128)(2,1)} fusion(bf16[1,64,5120]{2,1,0:T(8,128)(2,1)S(1)} %copy-done, bf16[1,32,5120]{2,1,0:T(8,128)(2,1)} %all-reduce.2.cloned.1.call-done, f32[32]{0:T(128)S(1)} %add_rsqrt_fusion.1), kind=kOutput, calls=%fused_computation.32 | convolution fusion | flops 21465088 | bytes 987264 | tf_op jit(solution)/shard_map/mtd,jd->mtj/dot_general | solution.py:99
  (55 shorter events, 10.9 us)
Async XLA Ops:
  6.5 121.6 %copy-start = (bf16[1,64,5120]{2,1,0:T(8,128)(2,1)S(1)}, bf16[1,64,5120]{2,1,0:T(8,128)(2,1)}, u32[]{:S(2)}) copy-start(bf16[1,64,5120]{2,1,0:T(8,128)(2,1)} %param.13) | copy-start | bytes 1966084
  6.5 120.4 %all-reduce.2.cloned.1.call-start = ((), (), s32[]{:S(2)}) async-start(), calls=%async_computation.2 | async-start | bytes 655360 | tf_op jit(solution)/shard_map/psum | solution.py:17
  7.7 26.5 %copy-start.1 = (bf16[1,192,5120]{2,1,0:T(8,128)(2,1)S(1)}, bf16[1,192,5120]{2,1,0:T(8,128)(2,1)}, u32[]{:S(2)}) copy-start(bf16[1,192,5120]{2,1,0:T(8,128)(2,1)} %get-tuple-element.586) | copy-start | bytes 5898244 | tf_op jit(solution)/shard_map/while
  7.7 9.6 %collective-permute-start = (bf16[32,5120]{1,0:T(8,128)(2,1)S(1)}, bf16[32,5120]{1,0:T(8,128)(2,1)S(1)}, u32[]{:S(2)}, u32[]{:S(2)}) collective-permute-start(bf16[32,5120]{1,0:T(8,128)(2,1)S(1)} %broadcast_select_fusion.3), channel_id=1, source_target_pairs={{0,16},{1,17},{2,18},{3,19},{4,20},{5,21},{6,22},{7,23},{8,24},{9,... | collective-permute-start | bytes 983048 | tf_op jit(solution)/shard_map/while/body/eval_jaxpr/ppermute | solution.py:12
  34.2 10.5 %copy-start.4 = (bf16[1,5120,2]{1,2,0:T(2,128)(2,1)S(1)}, bf16[1,5120,2]{1,2,0:T(2,128)(2,1)}, u32[]{:S(2)}) copy-start(bf16[1,5120,2]{1,2,0:T(2,128)(2,1)} %get-tuple-element.583) | copy-start | bytes 61444 | tf_op jit(solution)/shard_map/while
  37.2 14.6 %copy-start.2 = (bf16[1,32,5120]{2,1,0:T(8,128)(2,1)S(1)}, bf16[1,32,5120]{2,1,0:T(8,128)(2,1)}, u32[]{:S(2)}) copy-start(bf16[1,32,5120]{2,1,0:T(8,128)(2,1)} %get-tuple-element.564) | copy-start | bytes 983044 | tf_op jit(solution)/shard_map/while
  39.4 11.9 %all-to-all-start.1 = ((bf16[16,2,2560]{2,1,0:T(2,128)(2,1)}), bf16[16,2,2560]{2,1,0:T(2,128)(2,1)S(1)}, u32[]{:S(2)}, u32[]{:S(2)}) async-start(bf16[16,2,2560]{2,1,0:T(2,128)(2,1)} %reshape.140), calls=%async_computation.1 | async-start | bytes 327680 | tf_op jit(solution)/shard_map/while/body/eval_jaxpr/all_to_all | solution.py:68
  53.5 0.7 copy-start.3
  54.2 26.6 %copy-start.1 = (bf16[1,192,5120]{2,1,0:T(8,128)(2,1)S(1)}, bf16[1,192,5120]{2,1,0:T(8,128)(2,1)}, u32[]{:S(2)}) copy-start(bf16[1,192,5120]{2,1,0:T(8,128)(2,1)} %get-tuple-element.586) | copy-start | bytes 5898244 | tf_op jit(solution)/shard_map/while
  55.3 11.5 %collective-permute-start = (bf16[32,5120]{1,0:T(8,128)(2,1)S(1)}, bf16[32,5120]{1,0:T(8,128)(2,1)S(1)}, u32[]{:S(2)}, u32[]{:S(2)}) collective-permute-start(bf16[32,5120]{1,0:T(8,128)(2,1)S(1)} %broadcast_select_fusion.3), channel_id=1, source_target_pairs={{0,16},{1,17},{2,18},{3,19},{4,20},{5,21},{6,22},{7,23},{8,24},{9,... | collective-permute-start | bytes 983048 | tf_op jit(solution)/shard_map/while/body/eval_jaxpr/ppermute | solution.py:12
  80.8 10.5 %copy-start.4 = (bf16[1,5120,2]{1,2,0:T(2,128)(2,1)S(1)}, bf16[1,5120,2]{1,2,0:T(2,128)(2,1)}, u32[]{:S(2)}) copy-start(bf16[1,5120,2]{1,2,0:T(2,128)(2,1)} %get-tuple-element.583) | copy-start | bytes 61444 | tf_op jit(solution)/shard_map/while
  83.9 14.6 %copy-start.2 = (bf16[1,32,5120]{2,1,0:T(8,128)(2,1)S(1)}, bf16[1,32,5120]{2,1,0:T(8,128)(2,1)}, u32[]{:S(2)}) copy-start(bf16[1,32,5120]{2,1,0:T(8,128)(2,1)} %get-tuple-element.564) | copy-start | bytes 983044 | tf_op jit(solution)/shard_map/while
  86.0 11.9 %all-to-all-start.1 = ((bf16[16,2,2560]{2,1,0:T(2,128)(2,1)}), bf16[16,2,2560]{2,1,0:T(2,128)(2,1)S(1)}, u32[]{:S(2)}, u32[]{:S(2)}) async-start(bf16[16,2,2560]{2,1,0:T(2,128)(2,1)} %reshape.140), calls=%async_computation.1 | async-start | bytes 327680 | tf_op jit(solution)/shard_map/while/body/eval_jaxpr/all_to_all | solution.py:68
  100.1 0.7 copy-start.3
Sparse Core Ops, SparseCore 0:
  101.7 25.2 all-reduce.1
where the time goes:
time: 139 us; the launch traced here: 137 us
  waiting for transfers between devices  51.7 us (37%)
  blocking collectives  24.6 us (18%)
  starting transfers between devices  18.1 us (13%)
  between operations  13.4 us (10%)
  matrix products  12.4 us (9%)
  other arithmetic  10.4 us (7%)
  local copies, waits for them, and re-layouts  6.15 us (4%)
    psum x1, waiting for transfers between devices, from_root(): return lax.psum(jnp.where(mine, x, jnp.zeros_like(x)), axis)  25.4 us
    all_to_all x2, blocking collectives, layer(): lax.all_to_all(copies, 'expert', split_axis=0, concat_axis=0, tiled=True)  24.6 us
    ppermute x2, waiting for transfers between devices, passed_along(): return lax.ppermute(x, axis, pairs)  13.7 us
    all_to_all x2, waiting for transfers between devices, layer(): lax.all_to_all(partials, 'expert', split_axis=0, concat_axis=0, tiled=True)  12.6 us
    all_to_all x2, starting transfers between devices, layer(): lax.all_to_all(partials, 'expert', split_axis=0, concat_axis=0, tiled=True)  10.7 us
    ppermute x2, starting transfers between devices, passed_along(): return lax.ppermute(x, axis, pairs)  7.39 us
    dot_general x2, matrix products, expert_rows(): jnp.dot(hidden, w_down[0], preferred_element_type=jnp.float32)  6.05 us
    while x24, local copies, waits for them, and re-layouts  3.7 us
  transfers between devices with their start and end apart: 5, of which 5 were waited for; matrix products, arithmetic and copies ran while one was open for 0% of the time, Pallas kernels for 0%

commit v1 on v0

v1 whole, which is shorter than its diff:
```python
import functools

import jax
import jax.numpy as jnp
from jax import lax
from jax.experimental import pallas as pl
from jax.experimental.pallas import tpu as pltpu
from jax.sharding import PartitionSpec as P

EPS = 1e-06
CUT = 8
MESH = pl.DeviceIdType.MESH
NT = (((1,), (1,)), ((), ()))


def kernel(
    sections, width, experts, x_hbm, router_hbm, up_hbm, down_hbm, picks_hbm, probe_hbm, out_ref,
    x_ref, up_ref, down_ref, probe_ref, lists, place, rows, picked, arrived, partial, returned,
    load_sem, list_send, list_recv, row_send, row_recv, part_send, part_recv,
):
    section = lax.axis_index("pipe")
    me = lax.axis_index("expert")
    tokens, features = x_ref.shape
    hidden_units = up_hbm.shape[0]
    piece = features // CUT
    group = width // experts
    slots = sections * experts
    expert = me // group
    barrier = pltpu.get_barrier_semaphore()

    def greet(step, carry):
        other = lax.rem(me + step, width)
        for far in range(sections):
            to = lax.rem(section + far, sections)
            pl.semaphore_signal(barrier, inc=1, device_id=(to, other), device_id_type=MESH)
        return carry

    for far in range(1, sections):
        to = lax.rem(section + far, sections)
        pl.semaphore_signal(barrier, inc=1, device_id=(to, me), device_id_type=MESH)
    lax.fori_loop(1, width, greet, 0)

    loads = [
        pltpu.make_async_copy(picks_hbm, lists.at[section], load_sem.at[0]),
        pltpu.make_async_copy(x_hbm, x_ref, load_sem.at[1]),
        pltpu.make_async_copy(up_hbm, up_ref.at[pl.ds(0, hidden_units)], load_sem.at[2]),
        pltpu.make_async_copy(
            router_hbm, up_ref.at[pl.ds(hidden_units, router_hbm.shape[0])], load_sem.at[3]
        ),
        pltpu.make_async_copy(down_hbm, down_ref, load_sem.at[4]),
        pltpu.make_async_copy(probe_hbm, probe_ref, load_sem.at[5]),
    ]
    for load in loads:
        load.start()
    loads[0].wait()
    loads[1].wait()

    def places_of(section_lists):
        wide = jnp.concatenate(
            [jnp.broadcast_to(section_lists[e : e + 1], (CUT, section_lists.shape[1]))
             for e in range(experts)], axis=0,
        )
        local = wide - me * tokens
        owned = (local >= 0) & (local < tokens)
        found = jnp.where(owned, local + 1, 0).astype(jnp.float32)
        return jnp.sum(found, axis=1, keepdims=True) - 1.0

    def select(places):
        height = experts * CUT
        token_id = lax.broadcasted_iota(jnp.int32, (height, tokens), 1).astype(jnp.float32)
        cut_id = lax.rem(lax.broadcasted_iota(jnp.int32, (height, tokens), 0), CUT)
        hot = places == token_id
        total = jnp.zeros((height, piece), jnp.float32)
        for c in range(CUT):
            pick = jnp.where(hot & (cut_id == c), 1.0, 0.0).astype(jnp.bfloat16)
            total += jnp.dot(
                pick, x_ref[:, c * piece : (c + 1) * piece], preferred_element_type=jnp.float32
            )
        return total

    def note(which):
        places = places_of(lists[which])
        chosen = select(places)
        first = which * experts
        place[pl.ds(first, experts)] = jnp.broadcast_to(
            places, (experts * CUT, piece)
        ).reshape(experts, CUT, piece)
        rows[pl.ds(first, experts)] = chosen.reshape(experts, CUT, piece)

    note(section)

    def send_rows():
        picked[...] = rows[pl.ds(section * experts, experts)].astype(jnp.bfloat16)

        def send(step, carry):
            other = lax.rem(me + step, width)
            pltpu.make_async_remote_copy(
                src_ref=picked.at[other // group], dst_ref=arrived.at[me], send_sem=row_send,
                recv_sem=row_recv, device_id=(section, other), device_id_type=MESH,
            ).start()
            return carry

        lax.fori_loop(1, width, send, 0)
        pltpu.make_async_copy(picked.at[expert], arrived.at[me], row_recv).start()

    pl.semaphore_wait(barrier, sections * width - 1)

    @pl.when(section == 0)
    def _():
        send_rows()

    def list_copy(far):
        to = lax.rem(section + far, sections)
        return pltpu.make_async_remote_copy(
            src_ref=lists.at[section], dst_ref=lists.at[section], send_sem=list_send.at[far],
            recv_sem=list_recv.at[far], device_id=(to, me), device_id_type=MESH,
        )

    for far in range(1, sections):
        list_copy(far).start()

    loads[5].wait()
    x_all = x_ref[...]
    raw = lax.dot_general(x_all, probe_ref[...], NT, preferred_element_type=jnp.float32)
    x_wide = x_all.astype(jnp.float32)
    square = jnp.sum(x_wide * x_wide, axis=1, keepdims=True)
    base = raw * lax.rsqrt(square * (1.0 / features) + EPS)

    for far in range(1, sections):
        list_copy(far).wait()
        note(lax.rem(section + sections - far, sections))

    loads[2].wait()
    loads[3].wait()
    loads[4].wait()

    def over_cuts(value):
        count, lanes = value.shape
        summed = jnp.sum(value.reshape(count // CUT, CUT, lanes), axis=1, keepdims=True)
        return jnp.broadcast_to(summed, (count // CUT, CUT, lanes)).reshape(count, lanes)

    def expert_block():
        height = width * CUT
        wide = arrived[...].astype(jnp.float32).reshape(height, piece)
        narrow = wide.astype(jnp.bfloat16)
        mean = over_cuts(jnp.sum(wide * wide, axis=1, keepdims=True)) * (1.0 / features)
        scale = lax.rsqrt(mean + EPS)
        columns = up_ref.shape[0]
        cut_up = lax.rem(lax.broadcasted_iota(jnp.int32, (height, columns), 0), CUT)
        pre = jnp.zeros((height, columns), jnp.float32)
        for c in range(CUT):
            term = lax.dot_general(
                narrow, up_ref[:, c * piece : (c + 1) * piece], NT,
                preferred_element_type=jnp.float32,
            )
            pre = jnp.where(cut_up == c, term, pre)
        pre = over_cuts(pre) * scale
        column = lax.broadcasted_iota(jnp.int32, (height, columns), 1)
        logit = jnp.sum(
            jnp.where(column == hidden_units + expert, pre, 0.0), axis=1, keepdims=True
        )
        value = pre[:, :hidden_units]
        gate = 1.0 / (1.0 + jnp.exp(-logit))
        hidden = value / (1.0 + jnp.exp(-value)) * gate
        cut_down = lax.rem(lax.broadcasted_iota(jnp.int32, (height, hidden_units), 0), CUT)
        total = jnp.zeros((height, piece), jnp.float32)
        for c in range(CUT):
            masked = jnp.where(cut_down == c, hidden, 0.0).astype(jnp.bfloat16)
            total += jnp.dot(
                masked, down_ref[:, c * piece : (c + 1) * piece],
                preferred_element_type=jnp.float32,
            )
        partial[...] = total.reshape(width, CUT, piece).astype(jnp.bfloat16)

    def send_parts(phase):
        def give(owner, far):
            to = lax.rem(section + far, sections)
            pltpu.make_async_remote_copy(
                src_ref=partial.at[owner], dst_ref=returned.at[phase, me],
                send_sem=part_send.at[far], recv_sem=part_recv.at[phase],
                device_id=(to, owner), device_id_type=MESH,
            ).start()

        def send(step, carry):
            owner = lax.rem(me + step, width)
            for far in reversed(range(sections)):
                give(owner, far)
            return carry

        lax.fori_loop(1, width, send, 0)
        for far in range(1, sections):
            give(me, far)
        pltpu.make_async_copy(partial.at[me], returned.at[phase, me], part_recv.at[phase]).start()

    def phase_step(phase, carry):
        @pl.when(section == phase)
        def _():
            @pl.when(phase > 0)
            def _():
                send_rows()

            pltpu.make_async_copy(arrived, arrived, row_recv).wait()
            expert_block()
            send_parts(phase)

        pltpu.make_async_copy(returned.at[phase], returned.at[phase], part_recv.at[phase]).wait()
        updates = [
            jnp.sum(
                returned[phase, pl.ds(e * group, group)].astype(jnp.float32), axis=0
            )
            for e in range(experts)
        ]

        def apply(slot, inner):
            total = jnp.zeros((CUT, piece), jnp.float32)
            for e in range(experts):
                same = place[slot] == place[phase * experts + e]
                total += jnp.where(same, updates[e], 0.0)
            rows[slot] = (rows[slot] + total).astype(jnp.bfloat16).astype(jnp.float32)
            return inner

        lax.fori_loop(0, slots, apply, 0, unroll=slots <= 8)
        return carry

    lax.fori_loop(0, sections, phase_step, 0)

    height = slots * CUT
    wide = rows[...].reshape(height, piece)
    mean = over_cuts(jnp.sum(wide * wide, axis=1, keepdims=True)) * (1.0 / features)
    narrow = wide.astype(jnp.bfloat16)
    feats = probe_ref.shape[0]
    cut_out = lax.rem(lax.broadcasted_iota(jnp.int32, (height, feats), 0), CUT)
    changed = jnp.zeros((height, feats), jnp.float32)
    for c in range(CUT):
        term = lax.dot_general(
            narrow, probe_ref[:, c * piece : (c + 1) * piece], NT,
            preferred_element_type=jnp.float32,
        )
        changed = jnp.where(cut_out == c, term, changed)
    changed = over_cuts(changed) * lax.rsqrt(mean + EPS)
    token_id = lax.broadcasted_iota(jnp.int32, (tokens, feats), 0).astype(jnp.float32)
    result = base
    for slot in range(slots):
        at = place[slot][:1, :feats]
        result = jnp.where(token_id == at, changed[slot * CUT : slot * CUT + 1], result)
    out_ref[...] = result.astype(out_ref.dtype)

    for far in range(1, sections):
        pltpu.make_async_copy(returned.at[0], returned.at[0], part_send.at[far]).wait()
    most = returned.at[0, pl.ds(0, width - 1)]
    pltpu.make_async_copy(most, most, part_send.at[0]).wait()
    pltpu.make_async_copy(most, most, row_send).wait()


def shards(inputs, router, w_up, w_down, picks, probe):
    sections = lax.axis_size("pipe")
    width = lax.axis_size("expert")
    tokens, features = inputs.shape[1:]
    experts = router.shape[2]
    cap = picks.shape[3]
    hidden_units = w_up.shape[1]
    feats = probe.shape[1]
    piece = features // CUT
    padded = -(-experts // 16) * 16
    scorer = jnp.pad(jnp.transpose(router[0]), ((0, padded - experts), (0, 0)))
    slots = sections * experts
    any_spec = pl.BlockSpec(memory_space=pl.ANY)
    out = pl.pallas_call(
        functools.partial(kernel, sections, width, experts),
        out_shape=jax.ShapeDtypeStruct((tokens, feats), jnp.bfloat16),
        in_specs=[any_spec] * 6,
        out_specs=pl.BlockSpec(memory_space=pltpu.VMEM),
        scratch_shapes=[
            pltpu.VMEM((tokens, features), jnp.bfloat16),
            pltpu.VMEM((hidden_units + padded, features), jnp.bfloat16),
            pltpu.VMEM((hidden_units, features), jnp.bfloat16),
            pltpu.VMEM((feats, features), jnp.bfloat16),
            pltpu.VMEM((sections, experts, cap), jnp.int32),
            pltpu.VMEM((slots, CUT, piece), jnp.float32),
            pltpu.VMEM((slots, CUT, piece), jnp.float32),
            pltpu.VMEM((experts, CUT, piece), jnp.bfloat16),
            pltpu.VMEM((width, CUT, piece), jnp.bfloat16),
            pltpu.VMEM((width, CUT, piece), jnp.bfloat16),
            pltpu.VMEM((sections, width, CUT, piece), jnp.bfloat16),
            pltpu.SemaphoreType.DMA((6,)),
            pltpu.SemaphoreType.DMA((sections,)),
            pltpu.SemaphoreType.DMA((sections,)),
            pltpu.SemaphoreType.DMA,
            pltpu.SemaphoreType.DMA,
            pltpu.SemaphoreType.DMA((sections,)),
            pltpu.SemaphoreType.DMA((sections,)),
        ],
        compiler_params=pltpu.CompilerParams(collective_id=0, has_side_effects=True),
        name="relay",
    )(inputs[0], scorer, w_up[0], w_down[0], picks[0, 0], probe[0])
    return out[None, None]


def solution(mesh):
    return jax.shard_map(
        shards,
        mesh=mesh,
        in_specs=(
            P(None, "expert", None),
            P("pipe", None, None),
            P("pipe", "expert", None),
            P("pipe", "expert", None),
            P("pipe", None, None, None),
            P("pipe", None, None),
        ),
        out_specs=P("pipe", None, "expert", None),
        check_vma=False,
    )
```

time: 139 us -> 41.7 us (0.30); the launches traced: 137 us -> 41.5 us
  waiting for transfers between devices: 51.7 us -> 0 us
  Pallas kernels: 0 us -> 38.8 us
  blocking collectives: 24.6 us -> 0 us
  starting transfers between devices: 18.1 us -> 0 us
  between operations: 13.4 us -> 0.01 us
  matrix products: 12.4 us -> 0 us
  other arithmetic: 10.4 us -> 0 us
  local copies, waits for them, and re-layouts: 6.15 us -> 2.69 us
    pallas_call x0 -> x1, Pallas kernels: none -> 38.8 us  [shards(): pl.pallas_call(functools.partial(kernel, sections, width, experts), out_s...]
    psum x1 -> x0, waiting for transfers between devices: 25.4 us -> none  [from_root(): return lax.psum(jnp.where(mine, x, jnp.zeros_like(x)), axis)]
    all_to_all x2 -> x0, blocking collectives: 24.6 us -> none  [layer(): lax.all_to_all(copies, 'expert', split_axis=0, concat_axis=0, tiled=True)]
    ppermute x2 -> x0, waiting for transfers between devices: 13.7 us -> none  [passed_along(): return lax.ppermute(x, axis, pairs)]
    all_to_all x2 -> x0, waiting for transfers between devices: 12.6 us -> none  [layer(): lax.all_to_all(partials, 'expert', split_axis=0, concat_axis=0, tiled=True)]
    dot_general x10 -> x0, matrix products: 12.4 us -> none  [the longest x2 6.05 us: expert_rows(): jnp.dot(hidden, w_down[0], preferred_element_type=jnp.float32)]
    all_to_all x2 -> x0, starting transfers between devices: 10.7 us -> none  [layer(): lax.all_to_all(partials, 'expert', split_axis=0, concat_axis=0, tiled=True)]
    ppermute x2 -> x0, starting transfers between devices: 7.39 us -> none  [passed_along(): return lax.ppermute(x, axis, pairs)]
  transfers between devices with their start and end apart: 5 -> 0, of which waited for: 5 -> 0; matrix products, arithmetic and copies ran while one was open for 0% -> 0% of each run, Pallas kernels for 0% -> 0%
where the time goes in v1:
time: 41.7 us; the launch traced here: 41.5 us
  Pallas kernels  38.8 us (93%)
  local copies, waits for them, and re-layouts  2.69 us (6%)
    pallas_call x1, Pallas kernels, shards(): pl.pallas_call(functools.partial(kernel, sections, width, experts), out_s...  38.8 us
    pad x1, local copies, waits for them, and re-layouts, shards(): scorer = jnp.pad(jnp.transpose(router[0]), ((0, padded - experts), (0, 0)))  1.4 us
    unnamed x1, local copies, waits for them, and re-layouts  1.3 us

profile of v1, /device:TPU:9, one launch (start us, length us, event | category | flops | bytes accessed | tf_op | source)
XLA Modules:
  0.0 41.5 jit_solution(15444830589605848905)
XLA Ops:
  0.0 1.4 %pad.4.router_hbm = bf16[16,5120]{1,0:T(8,128)(2,1)} pad(bf16[2,5120]{1,0:T(2,128)(2,1)} %bitcast.14, bf16[]{:T(256)} %constant.2.clone.1), padding=0_14x0_0 | pad | bytes 184322 | tf_op jit(solution)/shard_map/jit(_pad)/pad | solution.py:265
  1.4 38.8 %relay.1 = bf16[32,64]{1,0:T(8,128)(2,1)} custom-call(bf16[32,5120]{1,0:T(8,128)(2,1)} %bitcast.12, bf16[16,5120]{1,0:T(8,128)(2,1)} %pad.4.router_hbm, bf16[192,5120]{1,0:T(8,128)(2,1)} %bitcast.9, bf16[192,5120]{1,0:T(8,128)(2,1)} %bitcast.10, s32[2,8]{1,0:T(2,128)} %bitcast.15, bf16[64,5120]{1,0:T(8,128)(2,1)} %bitcast.11), custom_call_target="tpu_custom_call" | custom-call | tf_op jit(solution)/shard_map/relay/pallas_call | solution.py:268
  40.2 1.3 %copy.8 = bf16[1,1,32,64]{3,2,1,0:T(8,128)(2,1)} copy(bf16[1,1,32,64]{3,2,1,0:T(8,128)(2,1)} %bitcast.13) | data formatting | bytes 8192

commit v2 on v1

v2 whole, which is shorter than its diff:
```python
import functools

import jax
import jax.numpy as jnp
from jax import lax
from jax.experimental import pallas as pl
from jax.experimental.pallas import tpu as pltpu
from jax.sharding import PartitionSpec as P

EPS = 1e-06
CUT = 8
PAD = 16
MESH = pl.DeviceIdType.MESH
NT = (((1,), (1,)), ((), ()))


def kernel(
    sections, width, experts, x_hbm, router_hbm, up_hbm, down_hbm, picks_hbm, probe_hbm, out_ref,
    x_ref, up_ref, down_ref, probe_ref, scorer, lists, place, rows, picked, arrived, stage,
    partial, returned, state_out, state_in, load_sem, list_send, list_recv, row_send, row_recv,
    part_send, part_recv, state_send, state_recv,
):
    section = lax.axis_index("pipe")
    me = lax.axis_index("expert")
    tokens, features = x_ref.shape
    hidden_units = up_hbm.shape[0]
    piece = features // CUT
    group = width // experts
    slots = sections * experts
    expert = me // group
    barrier = pltpu.get_barrier_semaphore()

    def around(step):
        index = me + step
        return jnp.where(index >= width, index - width, index)

    def far_pipe(far):
        index = section + far
        return jnp.where(index >= sections, index - sections, index)

    def expert_of(index):
        owner = jnp.int32(0)
        for e in range(1, experts):
            owner = owner + (index >= e * group).astype(jnp.int32)
        return owner

    steps = sorted(range(1, width), key=lambda step: -min(step, width - step))

    def each_step(act):
        if width <= 16:
            for step in steps:
                act(step)
        else:
            lax.fori_loop(1, width, lambda step, carry: (act(step), carry)[1], 0)

    def greet(step):
        other = around(step)
        for far in range(sections):
            to = far_pipe(far)
            pl.semaphore_signal(barrier, inc=1, device_id=(to, other), device_id_type=MESH)

    for far in range(1, sections):
        to = far_pipe(far)
        pl.semaphore_signal(barrier, inc=1, device_id=(to, me), device_id_type=MESH)
    each_step(greet)

    loads = [
        pltpu.make_async_copy(picks_hbm, lists.at[section], load_sem.at[0]),
        pltpu.make_async_copy(x_hbm, x_ref, load_sem.at[1]),
        pltpu.make_async_copy(up_hbm, up_ref.at[pl.ds(0, hidden_units)], load_sem.at[2]),
        pltpu.make_async_copy(router_hbm, scorer, load_sem.at[3]),
        pltpu.make_async_copy(down_hbm, down_ref, load_sem.at[4]),
        pltpu.make_async_copy(probe_hbm, probe_ref, load_sem.at[5]),
    ]
    for load in loads:
        load.start()
    loads[0].wait()
    loads[1].wait()

    def places_of(section_lists):
        wide = jnp.concatenate(
            [jnp.broadcast_to(section_lists[e : e + 1], (CUT, section_lists.shape[1]))
             for e in range(experts)], axis=0,
        )
        local = wide - me * tokens
        owned = (local >= 0) & (local < tokens)
        found = jnp.where(owned, local + 1, 0).astype(jnp.float32)
        return jnp.sum(found, axis=1, keepdims=True) - 1.0

    def select(places):
        height = experts * CUT
        token_id = lax.broadcasted_iota(jnp.int32, (height, tokens), 1).astype(jnp.float32)
        cut_id = lax.rem(lax.broadcasted_iota(jnp.int32, (height, tokens), 0), CUT)
        hot = places == token_id
        total = jnp.zeros((height, piece), jnp.float32)
        for c in range(CUT):
            pick = jnp.where(hot & (cut_id == c), 1.0, 0.0).astype(jnp.bfloat16)
            total += jnp.dot(
                pick, x_ref[:, c * piece : (c + 1) * piece], preferred_element_type=jnp.float32
            )
        return total

    def note(which):
        places = places_of(lists[which])
        chosen = select(places)
        first = which * experts
        place[pl.ds(first, experts)] = jnp.broadcast_to(
            places, (experts * CUT, piece)
        ).reshape(experts, CUT, piece)
        rows[pl.ds(first, experts)] = chosen.reshape(experts, CUT, piece)

    note(section)

    def send_rows():
        picked[...] = rows[pl.ds(section * experts, experts)].astype(jnp.bfloat16)

        def send(step):
            other = around(step)
            pltpu.make_async_remote_copy(
                src_ref=picked.at[expert_of(other)], dst_ref=arrived.at[me], send_sem=row_send,
                recv_sem=row_recv, device_id=(section, other), device_id_type=MESH,
            ).start()

        each_step(send)
        pltpu.make_async_copy(picked.at[expert], arrived.at[me], row_recv).start()

    pl.semaphore_wait(barrier, sections * width - 1)

    @pl.when(section == 0)
    def _():
        send_rows()

    def list_copy(far):
        to = far_pipe(far)
        return pltpu.make_async_remote_copy(
            src_ref=lists.at[section], dst_ref=lists.at[section], send_sem=list_send.at[far],
            recv_sem=list_recv.at[far], device_id=(to, me), device_id_type=MESH,
        )

    for far in range(1, sections):
        list_copy(far).start()

    loads[5].wait()
    x_all = x_ref[...]
    raw = lax.dot_general(x_all, probe_ref[...], NT, preferred_element_type=jnp.float32)
    x_wide = x_all.astype(jnp.float32)
    square = jnp.sum(x_wide * x_wide, axis=1, keepdims=True)
    base = raw * lax.rsqrt(square * (1.0 / features) + EPS)

    for far in range(1, sections):
        list_copy(far).wait()
        note(lax.rem(section + sections - far, sections))

    loads[2].wait()
    loads[3].wait()
    up_ref[pl.ds(hidden_units, PAD)] = jnp.zeros((PAD, features), jnp.bfloat16)
    up_ref[pl.ds(hidden_units, experts)] = scorer[...]
    loads[4].wait()

    def over_cuts(value):
        count, lanes = value.shape
        summed = jnp.sum(value.reshape(count // CUT, CUT, lanes), axis=1, keepdims=True)
        return jnp.broadcast_to(summed, (count // CUT, CUT, lanes)).reshape(count, lanes)

    def expert_block():
        wide = arrived[...].astype(jnp.float32).reshape(width * CUT, piece)
        lanes = stage.shape[2]
        for t in range(piece // lanes):
            stage[t] = wide[:, t * lanes : (t + 1) * lanes]
        squares = jnp.sum((wide * wide).reshape(width, CUT, piece), axis=1)
        scale = lax.rsqrt(jnp.sum(squares, axis=1, keepdims=True) * (1.0 / features) + EPS)
        columns = up_ref.shape[0]
        pre = jnp.zeros((width, columns), jnp.float32)
        for c in range(CUT):
            pre += lax.dot_general(
                jnp.concatenate(
                    [stage[t, pl.ds(c, width, stride=CUT)] for t in range(piece // lanes)], axis=1
                ).astype(jnp.bfloat16),
                up_ref[:, c * piece : (c + 1) * piece], NT,
                preferred_element_type=jnp.float32,
            )
        pre = pre * scale
        column = lax.broadcasted_iota(jnp.int32, (width, columns), 1)
        logit = jnp.sum(
            jnp.where(column == hidden_units + expert, pre, 0.0), axis=1, keepdims=True
        )
        value = pre[:, :hidden_units]
        gate = 1.0 / (1.0 + jnp.exp(-logit))
        hidden = (value / (1.0 + jnp.exp(-value)) * gate).astype(jnp.bfloat16)
        for c in range(CUT):
            block = jnp.dot(
                hidden, down_ref[:, c * piece : (c + 1) * piece],
                preferred_element_type=jnp.float32,
            )
            for t in range(piece // lanes):
                stage[t, pl.ds(c, width, stride=CUT)] = block[:, t * lanes : (t + 1) * lanes]
        for t in range(piece // lanes):
            partial[:, :, t * lanes : (t + 1) * lanes] = (
                stage[t].reshape(width, CUT, lanes).astype(jnp.bfloat16)
            )

    def give(owner, far, batch):
        pltpu.make_async_remote_copy(
            src_ref=partial.at[owner], dst_ref=returned.at[batch, me],
            send_sem=part_send.at[far], recv_sem=part_recv.at[batch],
            device_id=(far_pipe(far), owner), device_id_type=MESH,
        ).start()

    def pass_parts():
        each_step(lambda step: give(around(step), 1, 0))
        give(me, 1, 0)

    def share_parts():
        def send(step):
            for far in reversed(range(sections)):
                give(around(step), far, 1)

        each_step(send)
        for far in range(1, sections):
            give(me, far, 1)
        pltpu.make_async_copy(partial.at[me], returned.at[1, me], part_recv.at[1]).start()

    def give_state(far, batch):
        return pltpu.make_async_remote_copy(
            src_ref=state_out, dst_ref=state_in.at[batch], send_sem=state_send.at[far],
            recv_sem=state_recv.at[batch], device_id=(far_pipe(far), me), device_id_type=MESH,
        )

    def take_state(batch):
        pltpu.make_async_copy(state_in.at[batch], state_in.at[batch], state_recv.at[batch]).wait()
        rows[...] = state_in[batch].astype(jnp.float32)

    def take_parts(phase, batch):
        pltpu.make_async_copy(returned.at[batch], returned.at[batch], part_recv.at[batch]).wait()
        updates = [
            jnp.sum(returned[batch, pl.ds(e * group, group)].astype(jnp.float32), axis=0)
            for e in range(experts)
        ]

        def apply(slot, carry):
            total = jnp.zeros((CUT, piece), jnp.float32)
            for e in range(experts):
                same = place[slot] == place[phase * experts + e]
                total += jnp.where(same, updates[e], 0.0)
            rows[slot] = (rows[slot] + total).astype(jnp.bfloat16).astype(jnp.float32)
            return carry

        lax.fori_loop(0, slots, apply, 0, unroll=slots <= 8)

    last = sections - 1

    @pl.when(section < last)
    def _():
        @pl.when(section > 0)
        def _():
            @pl.when(section > 1)
            def _():
                take_state(0)

            take_parts(section - 1, 0)
            send_rows()
            state_out[...] = rows[...].astype(jnp.bfloat16)
            give_state(1, 0).start()

        pltpu.make_async_copy(arrived, arrived, row_recv).wait()
        expert_block()
        pass_parts()

    @pl.when(section == last)
    def _():
        if last > 0:
            if last > 1:
                take_state(0)
            take_parts(section - 1, 0)
            send_rows()
            state_out[...] = rows[...].astype(jnp.bfloat16)
            for far in range(1, sections):
                give_state(far, 1).start()
        pltpu.make_async_copy(arrived, arrived, row_recv).wait()
        expert_block()
        share_parts()

    if last > 0:
        @pl.when(section < last)
        def _():
            take_state(1)

    take_parts(last, 1)

    height = slots * CUT
    wide = rows[...].reshape(height, piece)
    mean = over_cuts(jnp.sum(wide * wide, axis=1, keepdims=True)) * (1.0 / features)
    narrow = wide.astype(jnp.bfloat16)
    feats = probe_ref.shape[0]
    cut_out = lax.rem(lax.broadcasted_iota(jnp.int32, (height, feats), 0), CUT)
    changed = jnp.zeros((height, feats), jnp.float32)
    for c in range(CUT):
        term = lax.dot_general(
            narrow, probe_ref[:, c * piece : (c + 1) * piece], NT,
            preferred_element_type=jnp.float32,
        )
        changed = jnp.where(cut_out == c, term, changed)
    changed = over_cuts(changed) * lax.rsqrt(mean + EPS)
    token_id = lax.broadcasted_iota(jnp.int32, (tokens, feats), 0).astype(jnp.float32)
    result = base
    for slot in range(slots):
        at = place[slot][:1, :feats]
        result = jnp.where(token_id == at, changed[slot * CUT : slot * CUT + 1], result)
    out_ref[...] = result.astype(out_ref.dtype)

    most = returned.at[0, pl.ds(0, width - 1)]
    pltpu.make_async_copy(most, most, row_send).wait()

    @pl.when(section < last)
    def _():
        pltpu.make_async_copy(returned.at[0], returned.at[0], part_send.at[1 % sections]).wait()

        @pl.when(section > 0)
        def _():
            give_state(1, 0).wait_send()

    @pl.when(section == last)
    def _():
        pltpu.make_async_copy(most, most, part_send.at[0]).wait()
        for far in range(1, sections):
            pltpu.make_async_copy(returned.at[0], returned.at[0], part_send.at[far]).wait()
            give_state(far, 1).wait_send()


def shards(inputs, router, w_up, w_down, picks, probe):
    sections = lax.axis_size("pipe")
    width = lax.axis_size("expert")
    tokens, features = inputs.shape[1:]
    experts = router.shape[2]
    cap = picks.shape[3]
    hidden_units = w_up.shape[1]
    feats = probe.shape[1]
    piece = features // CUT
    slots = sections * experts
    any_spec = pl.BlockSpec(memory_space=pl.ANY)
    out = pl.pallas_call(
        functools.partial(kernel, sections, width, experts),
        out_shape=jax.ShapeDtypeStruct((tokens, feats), jnp.bfloat16),
        in_specs=[any_spec] * 6,
        out_specs=pl.BlockSpec(memory_space=pltpu.VMEM),
        scratch_shapes=[
            pltpu.VMEM((tokens, features), jnp.bfloat16),
            pltpu.VMEM((hidden_units + PAD, features), jnp.bfloat16),
            pltpu.VMEM((hidden_units, features), jnp.bfloat16),
            pltpu.VMEM((feats, features), jnp.bfloat16),
            pltpu.VMEM((experts, features), jnp.bfloat16),
            pltpu.VMEM((sections, experts, cap), jnp.int32),
            pltpu.VMEM((slots, CUT, piece), jnp.float32),
            pltpu.VMEM((slots, CUT, piece), jnp.float32),
            pltpu.VMEM((experts, CUT, piece), jnp.bfloat16),
            pltpu.VMEM((width, CUT, piece), jnp.bfloat16),
            pltpu.VMEM((piece // 128, width * CUT, 128), jnp.float32),
            pltpu.VMEM((width, CUT, piece), jnp.bfloat16),
            pltpu.VMEM((2, width, CUT, piece), jnp.bfloat16),
            pltpu.VMEM((slots, CUT, piece), jnp.bfloat16),
            pltpu.VMEM((2, slots, CUT, piece), jnp.bfloat16),
            pltpu.SemaphoreType.DMA((6,)),
            pltpu.SemaphoreType.DMA((sections,)),
            pltpu.SemaphoreType.DMA((sections,)),
            pltpu.SemaphoreType.DMA,
            pltpu.SemaphoreType.DMA,
            pltpu.SemaphoreType.DMA((sections,)),
            pltpu.SemaphoreType.DMA((2,)),
            pltpu.SemaphoreType.DMA((sections,)),
            pltpu.SemaphoreType.DMA((2,)),
        ],
        compiler_params=pltpu.CompilerParams(collective_id=0, has_side_effects=True),
        name="relay",
    )(inputs[0], jnp.transpose(router[0]), w_up[0], w_down[0], picks[0, 0], probe[0])
    return out[None, None]


def solution(mesh):
    return jax.shard_map(
        shards,
        mesh=mesh,
        in_specs=(
            P(None, "expert", None),
            P("pipe", None, None),
            P("pipe", "expert", None),
            P("pipe", "expert", None),
            P("pipe", None, None, None),
            P("pipe", None, None),
        ),
        out_specs=P("pipe", None, "expert", None),
        check_vma=False,
    )
```

time: 41.7 us -> 40.1 us (0.962)
  the two profiles are of different devices: /device:TPU:9 before, /device:TPU:0 now
where the time goes in v2:
time: 40.1 us; the launch traced here: 39.9 us
  Pallas kernels  38.6 us (96%)
  local copies, waits for them, and re-layouts  1.3 us (3%)
    pallas_call x1, Pallas kernels, shards(): pl.pallas_call(functools.partial(kernel, sections, width, experts), out_s...  38.6 us
    unnamed x1, local copies, waits for them, and re-layouts  1.3 us

profile of v2, /device:TPU:0, one launch (start us, length us, event | category | flops | bytes accessed | tf_op | source)
XLA Modules:
  0.0 39.9 jit_solution(5047852395811495201)
XLA Ops:
  0.0 38.6 %relay.1 = bf16[32,64]{1,0:T(8,128)(2,1)} custom-call(bf16[32,5120]{1,0:T(8,128)(2,1)} %bitcast.12, bf16[2,5120]{1,0:T(2,128)(2,1)} %bitcast.14, bf16[192,5120]{1,0:T(8,128)(2,1)} %bitcast.9, bf16[192,5120]{1,0:T(8,128)(2,1)} %bitcast.10, s32[2,8]{1,0:T(2,128)} %bitcast.15, bf16[64,5120]{1,0:T(8,128)(2,1)} %bitcast.11), custom_call_target="tpu_custom_call" | custom-call | tf_op jit(solution)/shard_map/relay/pallas_call | solution.py:341
  38.6 1.3 %copy.8 = bf16[1,1,32,64]{3,2,1,0:T(8,128)(2,1)} copy(bf16[1,1,32,64]{3,2,1,0:T(8,128)(2,1)} %bitcast.13) | data formatting | bytes 8192

commit v3 on v2

--- a/solution.py
+++ b/solution.py
@@ -10,6 +10,7 @@
 EPS = 1e-06
 CUT = 8
 PAD = 16
+JOIN = 2
 MESH = pl.DeviceIdType.MESH
 NT = (((1,), (1,)), ((), ()))
 
@@ -44,7 +45,7 @@
             owner = owner + (index >= e * group).astype(jnp.int32)
         return owner
 
-    steps = sorted(range(1, width), key=lambda step: -min(step, width - step))
+    steps = range(1, width)
 
     def each_step(act):
         if width <= 16:
@@ -171,12 +172,13 @@
         scale = lax.rsqrt(jnp.sum(squares, axis=1, keepdims=True) * (1.0 / features) + EPS)
         columns = up_ref.shape[0]
         pre = jnp.zeros((width, columns), jnp.float32)
-        for c in range(CUT):
+        for c in range(0, CUT, JOIN):
             pre += lax.dot_general(
                 jnp.concatenate(
-                    [stage[t, pl.ds(c, width, stride=CUT)] for t in range(piece // lanes)], axis=1
+                    [stage[t, pl.ds(c + i, width, stride=CUT)]
+                     for i in range(JOIN) for t in range(piece // lanes)], axis=1
                 ).astype(jnp.bfloat16),
-                up_ref[:, c * piece : (c + 1) * piece], NT,
+                up_ref[:, c * piece : (c + JOIN) * piece], NT,
                 preferred_element_type=jnp.float32,
             )
         pre = pre * scale
@@ -187,13 +189,15 @@
         value = pre[:, :hidden_units]
         gate = 1.0 / (1.0 + jnp.exp(-logit))
         hidden = (value / (1.0 + jnp.exp(-value)) * gate).astype(jnp.bfloat16)
-        for c in range(CUT):
+        for c in range(0, CUT, JOIN):
             block = jnp.dot(
-                hidden, down_ref[:, c * piece : (c + 1) * piece],
+                hidden, down_ref[:, c * piece : (c + JOIN) * piece],
                 preferred_element_type=jnp.float32,
             )
-            for t in range(piece // lanes):
-                stage[t, pl.ds(c, width, stride=CUT)] = block[:, t * lanes : (t + 1) * lanes]
+            for i in range(JOIN):
+                for t in range(piece // lanes):
+                    at = i * piece + t * lanes
+                    stage[t, pl.ds(c + i, width, stride=CUT)] = block[:, at : at + lanes]
         for t in range(piece // lanes):
             partial[:, :, t * lanes : (t + 1) * lanes] = (
                 stage[t].reshape(width, CUT, lanes).astype(jnp.bfloat16)

time: 40.1 us -> 36.9 us (0.920)
  the two profiles are of different devices: /device:TPU:0 before, /device:TPU:9 now
where the time goes in v3:
time: 36.9 us; the launch traced here: 36.7 us
  Pallas kernels  35.4 us (96%)
  local copies, waits for them, and re-layouts  1.3 us (4%)
    pallas_call x1, Pallas kernels, shards(): pl.pallas_call(functools.partial(kernel, sections, width, experts), out_s...  35.4 us
    unnamed x1, local copies, waits for them, and re-layouts  1.3 us

profile of v3, /device:TPU:9, one launch (start us, length us, event | category | flops | bytes accessed | tf_op | source)
XLA Modules:
  0.0 36.7 jit_solution(10382994997582575849)
XLA Ops:
  0.0 35.4 %relay.1 = bf16[32,64]{1,0:T(8,128)(2,1)} custom-call(bf16[32,5120]{1,0:T(8,128)(2,1)} %bitcast.12, bf16[2,5120]{1,0:T(2,128)(2,1)} %bitcast.14, bf16[192,5120]{1,0:T(8,128)(2,1)} %bitcast.9, bf16[192,5120]{1,0:T(8,128)(2,1)} %bitcast.10, s32[2,8]{1,0:T(2,128)} %bitcast.15, bf16[64,5120]{1,0:T(8,128)(2,1)} %bitcast.11), custom_call_target="tpu_custom_call" | custom-call | tf_op jit(solution)/shard_map/relay/pallas_call | solution.py:345
  35.4 1.3 %copy.8 = bf16[1,1,32,64]{3,2,1,0:T(8,128)(2,1)} copy(bf16[1,1,32,64]{3,2,1,0:T(8,128)(2,1)} %bitcast.13) | data formatting | bytes 8192

commit v4 on v3

--- a/solution.py
+++ b/solution.py
@@ -215,13 +215,10 @@
         give(me, 1, 0)
 
     def share_parts():
-        def send(step):
-            for far in reversed(range(sections)):
-                give(around(step), far, 1)
-
-        each_step(send)
-        for far in range(1, sections):
+        for far in reversed(range(1, sections)):
             give(me, far, 1)
+            each_step(lambda step: give(around(step), far, 1))
+        each_step(lambda step: give(around(step), 0, 1))
         pltpu.make_async_copy(partial.at[me], returned.at[1, me], part_recv.at[1]).start()
 
     def give_state(far, batch):

time: 36.9 us -> 36.8 us (level)
  the two profiles are of different devices: /device:TPU:9 before, /device:TPU:3 now
where the time goes in v4:
time: 36.8 us; the launch traced here: 36.6 us
  Pallas kernels  35.3 us (96%)
  local copies, waits for them, and re-layouts  1.3 us (4%)
    pallas_call x1, Pallas kernels, shards(): pl.pallas_call(functools.partial(kernel, sections, width, experts), out_s...  35.3 us
    unnamed x1, local copies, waits for them, and re-layouts  1.3 us

profile of v4, /device:TPU:3, one launch (start us, length us, event | category | flops | bytes accessed | tf_op | source)
XLA Modules:
  0.0 36.6 jit_solution(346806260566161726)
XLA Ops:
  0.0 35.3 %relay.1 = bf16[32,64]{1,0:T(8,128)(2,1)} custom-call(bf16[32,5120]{1,0:T(8,128)(2,1)} %bitcast.12, bf16[2,5120]{1,0:T(2,128)(2,1)} %bitcast.14, bf16[192,5120]{1,0:T(8,128)(2,1)} %bitcast.9, bf16[192,5120]{1,0:T(8,128)(2,1)} %bitcast.10, s32[2,8]{1,0:T(2,128)} %bitcast.15, bf16[64,5120]{1,0:T(8,128)(2,1)} %bitcast.11), custom_call_target="tpu_custom_call" | custom-call | tf_op jit(solution)/shard_map/relay/pallas_call | solution.py:342
  35.3 1.3 %copy.8 = bf16[1,1,32,64]{3,2,1,0:T(8,128)(2,1)} copy(bf16[1,1,32,64]{3,2,1,0:T(8,128)(2,1)} %bitcast.13) | data formatting | bytes 8192
